TPU v7x, 128 devices: a whole 4x4x4 slice. The times are simulated.
128 devices in a mesh: section: 8 (over x, core), tp: 16 (over z, y).
Axes of the slice: x: 4, y: 4, z: 4, core: 2. Of those that a mesh axis runs over, the one named last changes fastest.
Arguments:
- layer_inputs: bfloat16 [16, 512, 4096], P('section', None, 'tp'), may hold values from -6 to 6
- weights: bfloat16 [16, 4096, 4096], P('section', 'tp'), may hold values from -0.046875 to 0.046875
- input_basis: bfloat16 [16, 4096, 64], P('section', 'tp'), may hold values from -0.09375 to 0.09375
- output_basis: bfloat16 [16, 4096, 32], P('section', 'tp'), may hold values from -0.09375 to 0.09375
- queries: bfloat16 [16, 512, 2048], P('section', 'tp'), may hold values from -0.00390625 to 0.00390625
- top_cotangent: bfloat16 [512, 4096], replicated, may hold values from -6 to 6
- sequence_example: int32 [4], replicated, may hold values from 0 to 1
Outputs:
- scores: float32 [2, 512], P(None, 'tp')
All inputs are finite; a program needn't handle non-finite values.
Results may differ from a plain program's by a relative error of at most 0.0094.
Values may be sent and summed in bfloat16 or wider, within the bound.
No kernel may reach another device: no remote copies, remote signals or barrier semaphores. Data moves between devices by JAX's collectives and lax.ppermute only.
A program may use at most 64 MiB of HBM per device.

v0:
```python
import jax
import jax.numpy as jnp
from jax import lax
from jax.sharding import PartitionSpec as P

SEQLEN = 128
SEQ_MB = 1
MB = 4
EXAMPLES = 2


def from_behind(value, axis, by):
    size = lax.axis_size(axis)
    pairs = [(i, i + by) for i in range(size) if 0 <= i + by < size]
    return lax.ppermute(value, axis, pairs)


def silu_parts(values):
    floats = values.astype(jnp.float32)
    logistic = jax.nn.sigmoid(floats)
    return ((floats * logistic).astype(jnp.bfloat16), logistic * (1.0 + floats * (1.0 - logistic)))


def contract_columns(portion, matrix):
    return lax.dot_general(
        portion, matrix, (((1,), (1,)), ((), ())), preferred_element_type=jnp.float32
    )


def outer_rows(out_feats, in_feats):
    joined = out_feats[:, :, :, None] * in_feats[:, :, None, :]
    return joined.reshape(joined.shape[0], joined.shape[1], -1)


def shards(
    layer_inputs, weights, input_basis, output_basis, queries, top_cotangent, sequence_example
):
    section_count = lax.axis_size("section")
    section_rank = lax.axis_index("section")
    tp_rank = lax.axis_index("tp")
    width_local = layer_inputs.shape[2]
    width_full = weights.shape[2]
    total_tokens = layer_inputs.shape[1]
    block_rows = SEQ_MB * SEQLEN
    activated, slopes = silu_parts(layer_inputs)
    partial_in = jnp.einsum(
        "ltd,ldr->tlr", activated, input_basis, preferred_element_type=jnp.float32
    )
    in_feats = lax.psum(partial_in.reshape(total_tokens, -1), "tp").reshape(partial_in.shape)
    example_index = jnp.arange(EXAMPLES, dtype=jnp.int32)
    is_top = section_rank == section_count - 1

    def fold_lower(portion):
        return contract_columns(portion, weights[0])

    def tick(tick_index, state):
        outgoing, grads, stored = state
        micro_index = tick_index - (section_count - 1 - section_rank)
        valid = (micro_index >= 0) & (micro_index < MB)
        micro_clip = jnp.clip(micro_index, 0, MB - 1)
        first_row = micro_clip * block_rows
        slope_block = lax.dynamic_slice_in_dim(slopes, first_row, block_rows, 1)
        received = from_behind(outgoing, "section", -1)
        top_block = lax.dynamic_slice_in_dim(top_cotangent, first_row, block_rows, 0)
        upper_full = jnp.where(is_top, top_block, received)
        upper_own = lax.dynamic_slice_in_dim(upper_full, tp_rank * width_local, width_local, 1)
        upper_branch = lax.dot_general(
            upper_full, weights[1], (((1,), (1,)), ((), ())), preferred_element_type=jnp.float32
        )
        middle_own = (upper_own.astype(jnp.float32) + slope_block[1] * upper_branch).astype(
            jnp.bfloat16
        )
        lower_branch = fold_lower(lax.all_gather(middle_own, "tp", axis=1, tiled=True))
        lower_own = (middle_own.astype(jnp.float32) + slope_block[0] * lower_branch).astype(
            jnp.bfloat16
        )
        new_outgoing = lax.all_gather(lower_own, "tp", axis=1, tiled=True)
        cotangents = jnp.stack([middle_own, upper_own], 0)
        partial_out = jnp.einsum(
            "lrd,ldk->rlk", cotangents, output_basis, preferred_element_type=jnp.float32
        )
        out_feats = lax.psum(partial_out.reshape(block_rows, -1), "tp").reshape(partial_out.shape)
        in_block = lax.dynamic_slice_in_dim(in_feats, first_row, block_rows, 0)
        block_examples = jnp.repeat(
            lax.dynamic_slice_in_dim(sequence_example, micro_clip * SEQ_MB, SEQ_MB, 0), SEQLEN
        )
        selector = (example_index[:, None] == block_examples[None, :]).astype(
            jnp.float32
        ) * valid.astype(jnp.float32)
        grads = grads + jnp.einsum(
            "er,rlk->lek",
            selector,
            outer_rows(out_feats, in_block),
            precision=lax.Precision.HIGHEST,
        )
        return (new_outgoing, grads, stored)

    outgoing_init = jnp.zeros((block_rows, width_full), jnp.bfloat16)
    grads_init = jnp.zeros((2, EXAMPLES, queries.shape[2]), jnp.float32)
    stored_init = jnp.zeros((1,), jnp.bfloat16)
    final_out, grads, stored = lax.fori_loop(
        0, MB + section_count - 1, tick, (outgoing_init, grads_init, stored_init)
    )
    layer_scores = jnp.einsum(
        "lek,lqk->eq", grads, queries.astype(jnp.float32), precision=lax.Precision.HIGHEST
    )
    return lax.psum(layer_scores, "section")


def solution(mesh):
    placed = (
        P("section", None, "tp"),
        P("section", "tp", None),
        P("section", "tp", None),
        P("section", "tp", None),
        P("section", "tp", None),
        P(),
        P(),
    )
    return jax.shard_map(
        shards, mesh=mesh, in_specs=placed, out_specs=P(None, "tp"), check_vma=False
    )
```

profile of v0, /device:TPU:1, one launch (start us, length us, event | category | flops | bytes accessed | tf_op | source)
XLA Modules:
  0.0 1662.4 jit_solution(13824720775074881913)
XLA Ops:
  9.2 87.7 %all-reduce.2.cloned.1.call-done = f32[512,2,64]{0,2,1:T(8,128)} async-done(((f32[512,2,64]{0,2,1:T(8,128)}), f32[512,2,64]{0,2,1:T(8,128)}) %all-reduce.2.cloned.1.call-update) | async-done | bytes 262160 | tf_op jit(solution)/shard_map/psum | solution.py:49
  98.0 1529.4 %while.18 = (s32[]{:T(128)}, bf16[128,4096]{1,0:T(8,128)(2,1)}, f32[2,2,2048]{2,1,0:T(2,128)S(1)}, pred[]{:T(512)}, s32[]{:T(128)}, /*index=5*/bf16[512,4096]{1,...) while((s32[]{:T(128)}, bf16[128,4096]{1,0:T(8,128)(2,1)}, ...), condition=%wide.region_3.4_spmd.clone, body=%wide.region_1.3_spmd.clone.sunk | while | flops 555048960 | bytes 25986044 | solution.py:101
  120.3 40.6 %all-gather.3.cloned.1.call-done = bf16[128,4096]{1,0:T(8,128)(2,1)} async-done(((bf16[128,256]{1,0:T(8,128)(2,1)}), bf16[128,4096]{1,0:T(8,128)(2,1)}) %all-gather.3.cloned.1.call-update) | async-done | bytes 1048592 | tf_op jit(solution)/shard_map/while/body/eval_jaxpr/all_gather | solution.py:73
  166.6 58.4 %psum.31 = f32[128,2,32]{0,2,1:T(8,128)S(1)} all-reduce(f32[128,2,32]{0,2,1:T(8,128)S(1)} %convolution_bitcast_fusion.5), channel_id=1, replica_groups=mesh['section'=8,'tp'=16] {'tp'}, use_global_device_ids=true, to_apply=%region_2.2 | all-reduce | flops 8192 | bytes 65536 | tf_op jit(solution)/shard_map/while/body/eval_jaxpr/psum | solution.py:82
  263.3 37.6 %all-gather.3.cloned.1.call-done = bf16[128,4096]{1,0:T(8,128)(2,1)} async-done(((bf16[128,256]{1,0:T(8,128)(2,1)}), bf16[128,4096]{1,0:T(8,128)(2,1)}) %all-gather.3.cloned.1.call-update) | async-done | bytes 1048592 | tf_op jit(solution)/shard_map/while/body/eval_jaxpr/all_gather | solution.py:73
  306.6 58.4 %psum.31 = f32[128,2,32]{0,2,1:T(8,128)S(1)} all-reduce(f32[128,2,32]{0,2,1:T(8,128)S(1)} %convolution_bitcast_fusion.5), channel_id=1, replica_groups=mesh['section'=8,'tp'=16] {'tp'}, use_global_device_ids=true, to_apply=%region_2.2 | all-reduce | flops 8192 | bytes 65536 | tf_op jit(solution)/shard_map/while/body/eval_jaxpr/psum | solution.py:82
  367.3 17.7 %collective-permute-start = (bf16[128,4096]{1,0:T(8,128)(2,1)}, bf16[128,4096]{1,0:T(8,128)(2,1)S(1)}, u32[]{:S(2)}, u32[]{:S(2)}) collective-permute-start(bf16[128,4096]{1,0:T(8,128)(2,1)} %get-tuple-element.465), channel_id=1, source_target_pairs={{16,0},{32,16},{48,32},{64,48},{80,64},{96,80},{112,96},{17,1},{33... | collective-permute-start | bytes 3145736 | tf_op jit(solution)/shard_map/while/body/eval_jaxpr/ppermute | solution.py:15
  403.3 37.6 %all-gather.3.cloned.1.call-done = bf16[128,4096]{1,0:T(8,128)(2,1)} async-done(((bf16[128,256]{1,0:T(8,128)(2,1)}), bf16[128,4096]{1,0:T(8,128)(2,1)}) %all-gather.3.cloned.1.call-update) | async-done | bytes 1048592 | tf_op jit(solution)/shard_map/while/body/eval_jaxpr/all_gather | solution.py:73
  446.6 58.4 %psum.31 = f32[128,2,32]{0,2,1:T(8,128)S(1)} all-reduce(f32[128,2,32]{0,2,1:T(8,128)S(1)} %convolution_bitcast_fusion.5), channel_id=1, replica_groups=mesh['section'=8,'tp'=16] {'tp'}, use_global_device_ids=true, to_apply=%region_2.2 | all-reduce | flops 8192 | bytes 65536 | tf_op jit(solution)/shard_map/while/body/eval_jaxpr/psum | solution.py:82
  507.3 17.7 %collective-permute-start = (bf16[128,4096]{1,0:T(8,128)(2,1)}, bf16[128,4096]{1,0:T(8,128)(2,1)S(1)}, u32[]{:S(2)}, u32[]{:S(2)}) collective-permute-start(bf16[128,4096]{1,0:T(8,128)(2,1)} %get-tuple-element.465), channel_id=1, source_target_pairs={{16,0},{32,16},{48,32},{64,48},{80,64},{96,80},{112,96},{17,1},{33... | collective-permute-start | bytes 3145736 | tf_op jit(solution)/shard_map/while/body/eval_jaxpr/ppermute | solution.py:15
  543.4 37.6 %all-gather.3.cloned.1.call-done = bf16[128,4096]{1,0:T(8,128)(2,1)} async-done(((bf16[128,256]{1,0:T(8,128)(2,1)}), bf16[128,4096]{1,0:T(8,128)(2,1)}) %all-gather.3.cloned.1.call-update) | async-done | bytes 1048592 | tf_op jit(solution)/shard_map/while/body/eval_jaxpr/all_gather | solution.py:73
  586.7 58.4 %psum.31 = f32[128,2,32]{0,2,1:T(8,128)S(1)} all-reduce(f32[128,2,32]{0,2,1:T(8,128)S(1)} %convolution_bitcast_fusion.5), channel_id=1, replica_groups=mesh['section'=8,'tp'=16] {'tp'}, use_global_device_ids=true, to_apply=%region_2.2 | all-reduce | flops 8192 | bytes 65536 | tf_op jit(solution)/shard_map/while/body/eval_jaxpr/psum | solution.py:82
  647.3 17.7 %collective-permute-start = (bf16[128,4096]{1,0:T(8,128)(2,1)}, bf16[128,4096]{1,0:T(8,128)(2,1)S(1)}, u32[]{:S(2)}, u32[]{:S(2)}) collective-permute-start(bf16[128,4096]{1,0:T(8,128)(2,1)} %get-tuple-element.465), channel_id=1, source_target_pairs={{16,0},{32,16},{48,32},{64,48},{80,64},{96,80},{112,96},{17,1},{33... | collective-permute-start | bytes 3145736 | tf_op jit(solution)/shard_map/while/body/eval_jaxpr/ppermute | solution.py:15
  683.4 37.6 %all-gather.3.cloned.1.call-done = bf16[128,4096]{1,0:T(8,128)(2,1)} async-done(((bf16[128,256]{1,0:T(8,128)(2,1)}), bf16[128,4096]{1,0:T(8,128)(2,1)}) %all-gather.3.cloned.1.call-update) | async-done | bytes 1048592 | tf_op jit(solution)/shard_map/while/body/eval_jaxpr/all_gather | solution.py:73
  726.7 58.4 %psum.31 = f32[128,2,32]{0,2,1:T(8,128)S(1)} all-reduce(f32[128,2,32]{0,2,1:T(8,128)S(1)} %convolution_bitcast_fusion.5), channel_id=1, replica_groups=mesh['section'=8,'tp'=16] {'tp'}, use_global_device_ids=true, to_apply=%region_2.2 | all-reduce | flops 8192 | bytes 65536 | tf_op jit(solution)/shard_map/while/body/eval_jaxpr/psum | solution.py:82
  787.3 17.7 %collective-permute-start = (bf16[128,4096]{1,0:T(8,128)(2,1)}, bf16[128,4096]{1,0:T(8,128)(2,1)S(1)}, u32[]{:S(2)}, u32[]{:S(2)}) collective-permute-start(bf16[128,4096]{1,0:T(8,128)(2,1)} %get-tuple-element.465), channel_id=1, source_target_pairs={{16,0},{32,16},{48,32},{64,48},{80,64},{96,80},{112,96},{17,1},{33... | collective-permute-start | bytes 3145736 | tf_op jit(solution)/shard_map/while/body/eval_jaxpr/ppermute | solution.py:15
  823.4 37.6 %all-gather.3.cloned.1.call-done = bf16[128,4096]{1,0:T(8,128)(2,1)} async-done(((bf16[128,256]{1,0:T(8,128)(2,1)}), bf16[128,4096]{1,0:T(8,128)(2,1)}) %all-gather.3.cloned.1.call-update) | async-done | bytes 1048592 | tf_op jit(solution)/shard_map/while/body/eval_jaxpr/all_gather | solution.py:73
  866.7 58.4 %psum.31 = f32[128,2,32]{0,2,1:T(8,128)S(1)} all-reduce(f32[128,2,32]{0,2,1:T(8,128)S(1)} %convolution_bitcast_fusion.5), channel_id=1, replica_groups=mesh['section'=8,'tp'=16] {'tp'}, use_global_device_ids=true, to_apply=%region_2.2 | all-reduce | flops 8192 | bytes 65536 | tf_op jit(solution)/shard_map/while/body/eval_jaxpr/psum | solution.py:82
  927.4 17.7 %collective-permute-start = (bf16[128,4096]{1,0:T(8,128)(2,1)}, bf16[128,4096]{1,0:T(8,128)(2,1)S(1)}, u32[]{:S(2)}, u32[]{:S(2)}) collective-permute-start(bf16[128,4096]{1,0:T(8,128)(2,1)} %get-tuple-element.465), channel_id=1, source_target_pairs={{16,0},{32,16},{48,32},{64,48},{80,64},{96,80},{112,96},{17,1},{33... | collective-permute-start | bytes 3145736 | tf_op jit(solution)/shard_map/while/body/eval_jaxpr/ppermute | solution.py:15
  963.4 37.6 %all-gather.3.cloned.1.call-done = bf16[128,4096]{1,0:T(8,128)(2,1)} async-done(((bf16[128,256]{1,0:T(8,128)(2,1)}), bf16[128,4096]{1,0:T(8,128)(2,1)}) %all-gather.3.cloned.1.call-update) | async-done | bytes 1048592 | tf_op jit(solution)/shard_map/while/body/eval_jaxpr/all_gather | solution.py:73
  1006.7 58.4 %psum.31 = f32[128,2,32]{0,2,1:T(8,128)S(1)} all-reduce(f32[128,2,32]{0,2,1:T(8,128)S(1)} %convolution_bitcast_fusion.5), channel_id=1, replica_groups=mesh['section'=8,'tp'=16] {'tp'}, use_global_device_ids=true, to_apply=%region_2.2 | all-reduce | flops 8192 | bytes 65536 | tf_op jit(solution)/shard_map/while/body/eval_jaxpr/psum | solution.py:82
  1103.5 37.6 %all-gather.3.cloned.1.call-done = bf16[128,4096]{1,0:T(8,128)(2,1)} async-done(((bf16[128,256]{1,0:T(8,128)(2,1)}), bf16[128,4096]{1,0:T(8,128)(2,1)}) %all-gather.3.cloned.1.call-update) | async-done | bytes 1048592 | tf_op jit(solution)/shard_map/while/body/eval_jaxpr/all_gather | solution.py:73
  1146.8 58.4 %psum.31 = f32[128,2,32]{0,2,1:T(8,128)S(1)} all-reduce(f32[128,2,32]{0,2,1:T(8,128)S(1)} %convolution_bitcast_fusion.5), channel_id=1, replica_groups=mesh['section'=8,'tp'=16] {'tp'}, use_global_device_ids=true, to_apply=%region_2.2 | all-reduce | flops 8192 | bytes 65536 | tf_op jit(solution)/shard_map/while/body/eval_jaxpr/psum | solution.py:82
  1207.4 17.7 %collective-permute-start = (bf16[128,4096]{1,0:T(8,128)(2,1)}, bf16[128,4096]{1,0:T(8,128)(2,1)S(1)}, u32[]{:S(2)}, u32[]{:S(2)}) collective-permute-start(bf16[128,4096]{1,0:T(8,128)(2,1)} %get-tuple-element.465), channel_id=1, source_target_pairs={{16,0},{32,16},{48,32},{64,48},{80,64},{96,80},{112,96},{17,1},{33... | collective-permute-start | bytes 3145736 | tf_op jit(solution)/shard_map/while/body/eval_jaxpr/ppermute | solution.py:15
  1243.5 37.6 %all-gather.3.cloned.1.call-done = bf16[128,4096]{1,0:T(8,128)(2,1)} async-done(((bf16[128,256]{1,0:T(8,128)(2,1)}), bf16[128,4096]{1,0:T(8,128)(2,1)}) %all-gather.3.cloned.1.call-update) | async-done | bytes 1048592 | tf_op jit(solution)/shard_map/while/body/eval_jaxpr/all_gather | solution.py:73
  1286.8 58.4 %psum.31 = f32[128,2,32]{0,2,1:T(8,128)S(1)} all-reduce(f32[128,2,32]{0,2,1:T(8,128)S(1)} %convolution_bitcast_fusion.5), channel_id=1, replica_groups=mesh['section'=8,'tp'=16] {'tp'}, use_global_device_ids=true, to_apply=%region_2.2 | all-reduce | flops 8192 | bytes 65536 | tf_op jit(solution)/shard_map/while/body/eval_jaxpr/psum | solution.py:82
  1347.4 17.7 %collective-permute-start = (bf16[128,4096]{1,0:T(8,128)(2,1)}, bf16[128,4096]{1,0:T(8,128)(2,1)S(1)}, u32[]{:S(2)}, u32[]{:S(2)}) collective-permute-start(bf16[128,4096]{1,0:T(8,128)(2,1)} %get-tuple-element.465), channel_id=1, source_target_pairs={{16,0},{32,16},{48,32},{64,48},{80,64},{96,80},{112,96},{17,1},{33... | collective-permute-start | bytes 3145736 | tf_op jit(solution)/shard_map/while/body/eval_jaxpr/ppermute | solution.py:15
  1383.5 37.6 %all-gather.3.cloned.1.call-done = bf16[128,4096]{1,0:T(8,128)(2,1)} async-done(((bf16[128,256]{1,0:T(8,128)(2,1)}), bf16[128,4096]{1,0:T(8,128)(2,1)}) %all-gather.3.cloned.1.call-update) | async-done | bytes 1048592 | tf_op jit(solution)/shard_map/while/body/eval_jaxpr/all_gather | solution.py:73
  1426.8 58.4 %psum.31 = f32[128,2,32]{0,2,1:T(8,128)S(1)} all-reduce(f32[128,2,32]{0,2,1:T(8,128)S(1)} %convolution_bitcast_fusion.5), channel_id=1, replica_groups=mesh['section'=8,'tp'=16] {'tp'}, use_global_device_ids=true, to_apply=%region_2.2 | all-reduce | flops 8192 | bytes 65536 | tf_op jit(solution)/shard_map/while/body/eval_jaxpr/psum | solution.py:82
  1523.5 37.6 %all-gather.3.cloned.1.call-done = bf16[128,4096]{1,0:T(8,128)(2,1)} async-done(((bf16[128,256]{1,0:T(8,128)(2,1)}), bf16[128,4096]{1,0:T(8,128)(2,1)}) %all-gather.3.cloned.1.call-update) | async-done | bytes 1048592 | tf_op jit(solution)/shard_map/while/body/eval_jaxpr/all_gather | solution.py:73
  1566.8 58.4 %psum.31 = f32[128,2,32]{0,2,1:T(8,128)S(1)} all-reduce(f32[128,2,32]{0,2,1:T(8,128)S(1)} %convolution_bitcast_fusion.5), channel_id=1, replica_groups=mesh['section'=8,'tp'=16] {'tp'}, use_global_device_ids=true, to_apply=%region_2.2 | all-reduce | flops 8192 | bytes 65536 | tf_op jit(solution)/shard_map/while/body/eval_jaxpr/psum | solution.py:82
  1627.8 28.1 %psum.28 = f32[2,32]{1,0:T(2,128)} all-reduce(f32[2,32]{1,0:T(2,128)S(1)} %convolution_bitcast_fusion.3), channel_id=1, replica_groups=mesh['section'=8,'tp'=16] {'section'}, use_global_device_ids=true, to_apply=%region_4.5 | all-reduce | flops 64 | bytes 512 | tf_op jit(solution)/shard_map/psum | solution.py:107
  (217 shorter events, 348.6 us)
Async XLA Ops:
  6.5 90.4 %all-reduce.2.cloned.1.call-start = ((), (), s32[]{:S(2)}) async-start(), calls=%async_computation | async-start | bytes 524288 | tf_op jit(solution)/shard_map/psum | solution.py:49
  98.0 62.9 %all-gather.3.cloned.1.call-start = ((), (), s32[]{:S(2)}) async-start(), calls=%async_computation.1 | async-start | bytes 1114112 | tf_op jit(solution)/shard_map/while/body/eval_jaxpr/all_gather | solution.py:73
  120.2 106.9 %all-gather.5.cloned.1.call-start = ((), (), s32[]{:S(2)}) async-start(), calls=%async_computation.2 | async-start | bytes 1114112 | tf_op jit(solution)/shard_map/while/body/eval_jaxpr/all_gather | solution.py:77
  227.2 73.7 %all-gather.3.cloned.1.call-start = ((), (), s32[]{:S(2)}) async-start(), calls=%async_computation.1 | async-start | bytes 1114112 | tf_op jit(solution)/shard_map/while/body/eval_jaxpr/all_gather | solution.py:73
  263.3 103.9 %all-gather.5.cloned.1.call-start = ((), (), s32[]{:S(2)}) async-start(), calls=%async_computation.2 | async-start | bytes 1114112 | tf_op jit(solution)/shard_map/while/body/eval_jaxpr/all_gather | solution.py:77
  367.2 73.8 %all-gather.3.cloned.1.call-start = ((), (), s32[]{:S(2)}) async-start(), calls=%async_computation.1 | async-start | bytes 1114112 | tf_op jit(solution)/shard_map/while/body/eval_jaxpr/all_gather | solution.py:73
  367.3 31.4 %collective-permute-start = (bf16[128,4096]{1,0:T(8,128)(2,1)}, bf16[128,4096]{1,0:T(8,128)(2,1)S(1)}, u32[]{:S(2)}, u32[]{:S(2)}) collective-permute-start(bf16[128,4096]{1,0:T(8,128)(2,1)} %get-tuple-element.465), channel_id=1, source_target_pairs={{16,0},{32,16},{48,32},{64,48},{80,64},{96,80},{112,96},{17,1},{33... | collective-permute-start | bytes 3145736 | tf_op jit(solution)/shard_map/while/body/eval_jaxpr/ppermute | solution.py:15
  403.3 103.9 %all-gather.5.cloned.1.call-start = ((), (), s32[]{:S(2)}) async-start(), calls=%async_computation.2 | async-start | bytes 1114112 | tf_op jit(solution)/shard_map/while/body/eval_jaxpr/all_gather | solution.py:77
  507.2 73.8 %all-gather.3.cloned.1.call-start = ((), (), s32[]{:S(2)}) async-start(), calls=%async_computation.1 | async-start | bytes 1114112 | tf_op jit(solution)/shard_map/while/body/eval_jaxpr/all_gather | solution.py:73
  507.3 31.4 %collective-permute-start = (bf16[128,4096]{1,0:T(8,128)(2,1)}, bf16[128,4096]{1,0:T(8,128)(2,1)S(1)}, u32[]{:S(2)}, u32[]{:S(2)}) collective-permute-start(bf16[128,4096]{1,0:T(8,128)(2,1)} %get-tuple-element.465), channel_id=1, source_target_pairs={{16,0},{32,16},{48,32},{64,48},{80,64},{96,80},{112,96},{17,1},{33... | collective-permute-start | bytes 3145736 | tf_op jit(solution)/shard_map/while/body/eval_jaxpr/ppermute | solution.py:15
  543.3 103.9 %all-gather.5.cloned.1.call-start = ((), (), s32[]{:S(2)}) async-start(), calls=%async_computation.2 | async-start | bytes 1114112 | tf_op jit(solution)/shard_map/while/body/eval_jaxpr/all_gather | solution.py:77
  647.3 73.8 %all-gather.3.cloned.1.call-start = ((), (), s32[]{:S(2)}) async-start(), calls=%async_computation.1 | async-start | bytes 1114112 | tf_op jit(solution)/shard_map/while/body/eval_jaxpr/all_gather | solution.py:73
  647.3 31.4 %collective-permute-start = (bf16[128,4096]{1,0:T(8,128)(2,1)}, bf16[128,4096]{1,0:T(8,128)(2,1)S(1)}, u32[]{:S(2)}, u32[]{:S(2)}) collective-permute-start(bf16[128,4096]{1,0:T(8,128)(2,1)} %get-tuple-element.465), channel_id=1, source_target_pairs={{16,0},{32,16},{48,32},{64,48},{80,64},{96,80},{112,96},{17,1},{33... | collective-permute-start | bytes 3145736 | tf_op jit(solution)/shard_map/while/body/eval_jaxpr/ppermute | solution.py:15
  683.3 103.9 %all-gather.5.cloned.1.call-start = ((), (), s32[]{:S(2)}) async-start(), calls=%async_computation.2 | async-start | bytes 1114112 | tf_op jit(solution)/shard_map/while/body/eval_jaxpr/all_gather | solution.py:77
  787.3 73.8 %all-gather.3.cloned.1.call-start = ((), (), s32[]{:S(2)}) async-start(), calls=%async_computation.1 | async-start | bytes 1114112 | tf_op jit(solution)/shard_map/while/body/eval_jaxpr/all_gather | solution.py:73
  787.3 31.4 %collective-permute-start = (bf16[128,4096]{1,0:T(8,128)(2,1)}, bf16[128,4096]{1,0:T(8,128)(2,1)S(1)}, u32[]{:S(2)}, u32[]{:S(2)}) collective-permute-start(bf16[128,4096]{1,0:T(8,128)(2,1)} %get-tuple-element.465), channel_id=1, source_target_pairs={{16,0},{32,16},{48,32},{64,48},{80,64},{96,80},{112,96},{17,1},{33... | collective-permute-start | bytes 3145736 | tf_op jit(solution)/shard_map/while/body/eval_jaxpr/ppermute | solution.py:15
  823.4 103.9 %all-gather.5.cloned.1.call-start = ((), (), s32[]{:S(2)}) async-start(), calls=%async_computation.2 | async-start | bytes 1114112 | tf_op jit(solution)/shard_map/while/body/eval_jaxpr/all_gather | solution.py:77
  927.3 73.8 %all-gather.3.cloned.1.call-start = ((), (), s32[]{:S(2)}) async-start(), calls=%async_computation.1 | async-start | bytes 1114112 | tf_op jit(solution)/shard_map/while/body/eval_jaxpr/all_gather | solution.py:73
  927.4 31.4 %collective-permute-start = (bf16[128,4096]{1,0:T(8,128)(2,1)}, bf16[128,4096]{1,0:T(8,128)(2,1)S(1)}, u32[]{:S(2)}, u32[]{:S(2)}) collective-permute-start(bf16[128,4096]{1,0:T(8,128)(2,1)} %get-tuple-element.465), channel_id=1, source_target_pairs={{16,0},{32,16},{48,32},{64,48},{80,64},{96,80},{112,96},{17,1},{33... | collective-permute-start | bytes 3145736 | tf_op jit(solution)/shard_map/while/body/eval_jaxpr/ppermute | solution.py:15
  963.4 103.9 %all-gather.5.cloned.1.call-start = ((), (), s32[]{:S(2)}) async-start(), calls=%async_computation.2 | async-start | bytes 1114112 | tf_op jit(solution)/shard_map/while/body/eval_jaxpr/all_gather | solution.py:77
  1067.3 73.8 %all-gather.3.cloned.1.call-start = ((), (), s32[]{:S(2)}) async-start(), calls=%async_computation.1 | async-start | bytes 1114112 | tf_op jit(solution)/shard_map/while/body/eval_jaxpr/all_gather | solution.py:73
  1067.4 31.4 %collective-permute-start = (bf16[128,4096]{1,0:T(8,128)(2,1)}, bf16[128,4096]{1,0:T(8,128)(2,1)S(1)}, u32[]{:S(2)}, u32[]{:S(2)}) collective-permute-start(bf16[128,4096]{1,0:T(8,128)(2,1)} %get-tuple-element.465), channel_id=1, source_target_pairs={{16,0},{32,16},{48,32},{64,48},{80,64},{96,80},{112,96},{17,1},{33... | collective-permute-start | bytes 3145736 | tf_op jit(solution)/shard_map/while/body/eval_jaxpr/ppermute | solution.py:15
  1103.4 103.9 %all-gather.5.cloned.1.call-start = ((), (), s32[]{:S(2)}) async-start(), calls=%async_computation.2 | async-start | bytes 1114112 | tf_op jit(solution)/shard_map/while/body/eval_jaxpr/all_gather | solution.py:77
  1207.4 73.8 %all-gather.3.cloned.1.call-start = ((), (), s32[]{:S(2)}) async-start(), calls=%async_computation.1 | async-start | bytes 1114112 | tf_op jit(solution)/shard_map/while/body/eval_jaxpr/all_gather | solution.py:73
  1207.4 31.4 %collective-permute-start = (bf16[128,4096]{1,0:T(8,128)(2,1)}, bf16[128,4096]{1,0:T(8,128)(2,1)S(1)}, u32[]{:S(2)}, u32[]{:S(2)}) collective-permute-start(bf16[128,4096]{1,0:T(8,128)(2,1)} %get-tuple-element.465), channel_id=1, source_target_pairs={{16,0},{32,16},{48,32},{64,48},{80,64},{96,80},{112,96},{17,1},{33... | collective-permute-start | bytes 3145736 | tf_op jit(solution)/shard_map/while/body/eval_jaxpr/ppermute | solution.py:15
  1243.4 103.9 %all-gather.5.cloned.1.call-start = ((), (), s32[]{:S(2)}) async-start(), calls=%async_computation.2 | async-start | bytes 1114112 | tf_op jit(solution)/shard_map/while/body/eval_jaxpr/all_gather | solution.py:77
  1347.4 73.8 %all-gather.3.cloned.1.call-start = ((), (), s32[]{:S(2)}) async-start(), calls=%async_computation.1 | async-start | bytes 1114112 | tf_op jit(solution)/shard_map/while/body/eval_jaxpr/all_gather | solution.py:73
  1347.4 31.4 %collective-permute-start = (bf16[128,4096]{1,0:T(8,128)(2,1)}, bf16[128,4096]{1,0:T(8,128)(2,1)S(1)}, u32[]{:S(2)}, u32[]{:S(2)}) collective-permute-start(bf16[128,4096]{1,0:T(8,128)(2,1)} %get-tuple-element.465), channel_id=1, source_target_pairs={{16,0},{32,16},{48,32},{64,48},{80,64},{96,80},{112,96},{17,1},{33... | collective-permute-start | bytes 3145736 | tf_op jit(solution)/shard_map/while/body/eval_jaxpr/ppermute | solution.py:15
  1383.5 103.9 %all-gather.5.cloned.1.call-start = ((), (), s32[]{:S(2)}) async-start(), calls=%async_computation.2 | async-start | bytes 1114112 | tf_op jit(solution)/shard_map/while/body/eval_jaxpr/all_gather | solution.py:77
  1487.4 73.8 %all-gather.3.cloned.1.call-start = ((), (), s32[]{:S(2)}) async-start(), calls=%async_computation.1 | async-start | bytes 1114112 | tf_op jit(solution)/shard_map/while/body/eval_jaxpr/all_gather | solution.py:73
  1487.5 31.4 %collective-permute-start = (bf16[128,4096]{1,0:T(8,128)(2,1)}, bf16[128,4096]{1,0:T(8,128)(2,1)S(1)}, u32[]{:S(2)}, u32[]{:S(2)}) collective-permute-start(bf16[128,4096]{1,0:T(8,128)(2,1)} %get-tuple-element.465), channel_id=1, source_target_pairs={{16,0},{32,16},{48,32},{64,48},{80,64},{96,80},{112,96},{17,1},{33... | collective-permute-start | bytes 3145736 | tf_op jit(solution)/shard_map/while/body/eval_jaxpr/ppermute | solution.py:15
  1523.5 103.9 %all-gather.5.cloned.1.call-start = ((), (), s32[]{:S(2)}) async-start(), calls=%async_computation.2 | async-start | bytes 1114112 | tf_op jit(solution)/shard_map/while/body/eval_jaxpr/all_gather | solution.py:77
  (17 other events, 2329.2 us)
Sparse Core Ops, SparseCore 0:
  10.5 86.3 all-reduce.1
  120.3 40.5 all-gather.2
  164.4 42.9 all-gather.4
  263.4 37.5 all-gather.2
  304.4 42.9 all-gather.4
  403.4 37.5 all-gather.2
  444.4 42.9 all-gather.4
  543.4 37.5 all-gather.2
  584.5 42.9 all-gather.4
  683.4 37.5 all-gather.2
  724.5 42.9 all-gather.4
  823.5 37.5 all-gather.2
  864.5 42.9 all-gather.4
  963.5 37.5 all-gather.2
  1004.5 42.9 all-gather.4
  1103.5 37.5 all-gather.2
  1144.6 42.9 all-gather.4
  1243.5 37.5 all-gather.2
  1284.6 42.9 all-gather.4
  1383.6 37.5 all-gather.2
  1424.6 42.9 all-gather.4
  1523.6 37.5 all-gather.2
  1564.6 42.9 all-gather.4
where the time goes:
time: 1660 us
  blocking collectives  671 us (40%)
  waiting for transfers between devices  657 us (40%)
  starting transfers between devices  182 us (11%)
  matrix products  95 us (6%)
  other arithmetic  26.3 us (2%)
  local copies, waits for them, and re-layouts  17.8 us (1%)
    psum x11, blocking collectives, tick(): lax.psum(partial_out.reshape(block_rows, -1), 'tp')  643 us
    all_gather x11, waiting for transfers between devices, tick(): lax.all_gather(middle_own, 'tp', axis=1, tiled=True)  417 us
    ppermute x11, starting transfers between devices, from_behind(): return lax.ppermute(value, axis, pairs)  181 us
    ppermute x11, waiting for transfers between devices, from_behind(): return lax.ppermute(value, axis, pairs)  151 us
    psum x1, waiting for transfers between devices, shards(): lax.psum(partial_in.reshape(total_tokens, -1), 'tp')  87.7 us
    dot_general x11, matrix products, contract_columns(): lax.dot_general(portion, matrix, (((1,), (1,)), ((), ())), preferred_elem...  36.4 us
    dot_general x11, matrix products, tick(): lax.dot_general(upper_full, weights[1], (((1,), (1,)), ((), ())), preferr...  33.7 us
  transfers between devices with their start and end apart: 34, of which 23 were waited for; matrix products, arithmetic and copies ran while one was open for 3% of the time, Pallas kernels for 0%

commit v1 on v0

--- a/solution.py
+++ b/solution.py
@@ -7,6 +7,22 @@
 SEQ_MB = 1
 MB = 4
 EXAMPLES = 2
+
+
+def gather_around(x, axis, dim):
+    ways, here, hop = (lax.axis_size(axis), lax.axis_index(axis), x.shape[dim])
+    shape = [n * ways if d == dim else n for d, n in enumerate(x.shape)]
+    full = lax.dynamic_update_slice_in_dim(jnp.zeros(shape, x.dtype), x, here * hop, axis=dim)
+    going_up = going_down = x
+    for far in range(1, ways // 2 + 1):
+        going_up = lax.ppermute(going_up, axis, [(d, (d + 1) % ways) for d in range(ways)])
+        full = lax.dynamic_update_slice_in_dim(full, going_up, (here - far) % ways * hop, axis=dim)
+        if 2 * far < ways:
+            going_down = lax.ppermute(going_down, axis, [(d, (d - 1) % ways) for d in range(ways)])
+            full = lax.dynamic_update_slice_in_dim(
+                full, going_down, (here + far) % ways * hop, axis=dim
+            )
+    return full
 
 
 def from_behind(value, axis, by):
@@ -70,7 +86,7 @@
         middle_own = (upper_own.astype(jnp.float32) + slope_block[1] * upper_branch).astype(
             jnp.bfloat16
         )
-        lower_branch = fold_lower(lax.all_gather(middle_own, "tp", axis=1, tiled=True))
+        lower_branch = fold_lower(gather_around(middle_own, "tp", 1))
         lower_own = (middle_own.astype(jnp.float32) + slope_block[0] * lower_branch).astype(
             jnp.bfloat16
         )

time: 1660 us -> 1870 us (1.13)
  starting transfers between devices: 182 us -> 370 us
  waiting for transfers between devices: 657 us -> 687 us
  blocking collectives: 671 us -> 648 us
    all_gather x11 -> x0, waiting for transfers between devices: 417 us -> none  [tick(): lax.all_gather(middle_own, 'tp', axis=1, tiled=True)]
    ppermute x0 -> x165, starting transfers between devices: none -> 334 us  [the longest x77 319 us: gather_around(): lax.ppermute(going_down, axis, [(d, (d - 1) % ways) for d in range(ways)])]
    ppermute x0 -> x165, waiting for transfers between devices: none -> 244 us  [the longest x88 152 us: gather_around(): lax.ppermute(going_up, axis, [(d, (d + 1) % ways) for d in range(ways)])]
    ppermute x11, waiting for transfers between devices: 151 us -> 355 us  [from_behind(): return lax.ppermute(value, axis, pairs)]
    ppermute x11, starting transfers between devices: 181 us -> 35.7 us  [from_behind(): return lax.ppermute(value, axis, pairs)]
    psum x11, blocking collectives: 643 us -> 614 us  [tick(): lax.psum(partial_out.reshape(block_rows, -1), 'tp')]
  transfers between devices with their start and end apart: 34 -> 188, of which waited for: 23 -> 127; matrix products, arithmetic and copies ran while one was open for 3% -> 3% of each run, Pallas kernels for 0% -> 0%
where the time goes in v1:
time: 1870 us
  waiting for transfers between devices  687 us (37%)
  blocking collectives  648 us (35%)
  starting transfers between devices  370 us (20%)
  matrix products  85 us (5%)
  local copies, waits for them, and re-layouts  35.6 us (2%)
  other arithmetic  28.4 us (2%)
    psum x11, blocking collectives, tick(): lax.psum(partial_out.reshape(block_rows, -1), 'tp')  614 us
    ppermute x11, waiting for transfers between devices, from_behind(): return lax.ppermute(value, axis, pairs)  355 us
    ppermute x77, starting transfers between devices, gather_around(): lax.ppermute(going_down, axis, [(d, (d - 1) % ways) for d in range(ways)])  319 us
    ppermute x88, waiting for transfers between devices, gather_around(): lax.ppermute(going_up, axis, [(d, (d + 1) % ways) for d in range(ways)])  152 us
    ppermute x77, waiting for transfers between devices, gather_around(): lax.ppermute(going_down, axis, [(d, (d - 1) % ways) for d in range(ways)])  91.1 us
    psum x1, waiting for transfers between devices, shards(): lax.psum(partial_in.reshape(total_tokens, -1), 'tp')  87.7 us
  transfers between devices with their start and end apart: 188, of which 127 were waited for; matrix products, arithmetic and copies ran while one was open for 3% of the time, Pallas kernels for 0%

profile of v1, /device:TPU:1, one launch (start us, length us, event | category | flops | bytes accessed | tf_op | source)
XLA Modules:
  0.0 1869.8 jit_solution(1526520680369008243)
XLA Ops:
  9.2 87.7 %all-reduce.2.cloned.1.call-done = f32[512,2,64]{0,2,1:T(8,128)} async-done(((f32[512,2,64]{0,2,1:T(8,128)}), f32[512,2,64]{0,2,1:T(8,128)}) %all-reduce.2.cloned.1.call-update) | async-done | bytes 262160 | tf_op jit(solution)/shard_map/psum | solution.py:65
  98.0 1730.7 %while.18 = (s32[]{:T(128)}, bf16[128,4096]{1,0:T(8,128)(2,1)}, f32[2,2,2048]{2,1,0:T(2,128)}, pred[]{:T(512)}, s32[]{:T(128)}, /*index=5*/bf16[512,4096]{1,0:T(...) while((s32[]{:T(128)}, bf16[128,4096]{1,0:T(8,128)(2,1)}, ...), condition=%wide.region_3.4_spmd.clone, body=%wide.region_1.3_spmd.clone.sunk | while | flops 555048960 | bytes 46567168 | solution.py:117
  101.9 13.7 collective-permute-done
  181.1 56.2 %psum.32 = f32[128,2,32]{0,2,1:T(8,128)S(1)} all-reduce(f32[128,2,32]{0,2,1:T(8,128)S(1)} %convolution_bitcast_fusion.5), channel_id=1, replica_groups=mesh['section'=8,'tp'=16] {'tp'}, use_global_device_ids=true, to_apply=%region_2.2 | all-reduce | flops 8192 | bytes 65536 | tf_op jit(solution)/shard_map/while/body/eval_jaxpr/psum | solution.py:98
  240.1 13.4 collective-permute-start
  253.5 24.0 %collective-permute-done = bf16[128,4096]{1,0:T(8,128)(2,1)S(1)} collective-permute-done((bf16[128,4096]{1,0:T(8,128)(2,1)}, bf16[128,4096]{1,0:T(8,128)(2,1)S(1)}, u32[]{:S(2)}, u32[]{:S(2)}) %collective-permute-start) | collective-permute-done | bytes 1048608 | tf_op jit(solution)/shard_map/while/body/eval_jaxpr/ppermute | solution.py:31
  340.4 56.1 %psum.32 = f32[128,2,32]{0,2,1:T(8,128)S(1)} all-reduce(f32[128,2,32]{0,2,1:T(8,128)S(1)} %convolution_bitcast_fusion.5), channel_id=1, replica_groups=mesh['section'=8,'tp'=16] {'tp'}, use_global_device_ids=true, to_apply=%region_2.2 | all-reduce | flops 8192 | bytes 65536 | tf_op jit(solution)/shard_map/while/body/eval_jaxpr/psum | solution.py:98
  402.5 34.0 %collective-permute-done = bf16[128,4096]{1,0:T(8,128)(2,1)S(1)} collective-permute-done((bf16[128,4096]{1,0:T(8,128)(2,1)}, bf16[128,4096]{1,0:T(8,128)(2,1)S(1)}, u32[]{:S(2)}, u32[]{:S(2)}) %collective-permute-start) | collective-permute-done | bytes 1048608 | tf_op jit(solution)/shard_map/while/body/eval_jaxpr/ppermute | solution.py:31
  480.0 6.5 collective-permute-done.13
  499.3 55.8 %psum.32 = f32[128,2,32]{0,2,1:T(8,128)S(1)} all-reduce(f32[128,2,32]{0,2,1:T(8,128)S(1)} %convolution_bitcast_fusion.5), channel_id=1, replica_groups=mesh['section'=8,'tp'=16] {'tp'}, use_global_device_ids=true, to_apply=%region_2.2 | all-reduce | flops 8192 | bytes 65536 | tf_op jit(solution)/shard_map/while/body/eval_jaxpr/psum | solution.py:98
  559.8 36.0 %collective-permute-done = bf16[128,4096]{1,0:T(8,128)(2,1)S(1)} collective-permute-done((bf16[128,4096]{1,0:T(8,128)(2,1)}, bf16[128,4096]{1,0:T(8,128)(2,1)S(1)}, u32[]{:S(2)}, u32[]{:S(2)}) %collective-permute-start) | collective-permute-done | bytes 1048608 | tf_op jit(solution)/shard_map/while/body/eval_jaxpr/ppermute | solution.py:31
  646.0 6.6 collective-permute-done.15
  659.0 55.8 %psum.32 = f32[128,2,32]{0,2,1:T(8,128)S(1)} all-reduce(f32[128,2,32]{0,2,1:T(8,128)S(1)} %convolution_bitcast_fusion.5), channel_id=1, replica_groups=mesh['section'=8,'tp'=16] {'tp'}, use_global_device_ids=true, to_apply=%region_2.2 | all-reduce | flops 8192 | bytes 65536 | tf_op jit(solution)/shard_map/while/body/eval_jaxpr/psum | solution.py:98
  719.5 35.0 %collective-permute-done = bf16[128,4096]{1,0:T(8,128)(2,1)S(1)} collective-permute-done((bf16[128,4096]{1,0:T(8,128)(2,1)}, bf16[128,4096]{1,0:T(8,128)(2,1)S(1)}, u32[]{:S(2)}, u32[]{:S(2)}) %collective-permute-start) | collective-permute-done | bytes 1048608 | tf_op jit(solution)/shard_map/while/body/eval_jaxpr/ppermute | solution.py:31
  804.5 6.4 collective-permute-done.15
  817.2 55.7 %psum.32 = f32[128,2,32]{0,2,1:T(8,128)S(1)} all-reduce(f32[128,2,32]{0,2,1:T(8,128)S(1)} %convolution_bitcast_fusion.5), channel_id=1, replica_groups=mesh['section'=8,'tp'=16] {'tp'}, use_global_device_ids=true, to_apply=%region_2.2 | all-reduce | flops 8192 | bytes 65536 | tf_op jit(solution)/shard_map/while/body/eval_jaxpr/psum | solution.py:98
  877.6 35.8 %collective-permute-done = bf16[128,4096]{1,0:T(8,128)(2,1)S(1)} collective-permute-done((bf16[128,4096]{1,0:T(8,128)(2,1)}, bf16[128,4096]{1,0:T(8,128)(2,1)S(1)}, u32[]{:S(2)}, u32[]{:S(2)}) %collective-permute-start) | collective-permute-done | bytes 1048608 | tf_op jit(solution)/shard_map/while/body/eval_jaxpr/ppermute | solution.py:31
  976.3 56.2 %psum.32 = f32[128,2,32]{0,2,1:T(8,128)S(1)} all-reduce(f32[128,2,32]{0,2,1:T(8,128)S(1)} %convolution_bitcast_fusion.5), channel_id=1, replica_groups=mesh['section'=8,'tp'=16] {'tp'}, use_global_device_ids=true, to_apply=%region_2.2 | all-reduce | flops 8192 | bytes 65536 | tf_op jit(solution)/shard_map/while/body/eval_jaxpr/psum | solution.py:98
  1037.2 35.1 %collective-permute-done = bf16[128,4096]{1,0:T(8,128)(2,1)S(1)} collective-permute-done((bf16[128,4096]{1,0:T(8,128)(2,1)}, bf16[128,4096]{1,0:T(8,128)(2,1)S(1)}, u32[]{:S(2)}, u32[]{:S(2)}) %collective-permute-start) | collective-permute-done | bytes 1048608 | tf_op jit(solution)/shard_map/while/body/eval_jaxpr/ppermute | solution.py:31
  1134.8 55.7 %psum.32 = f32[128,2,32]{0,2,1:T(8,128)S(1)} all-reduce(f32[128,2,32]{0,2,1:T(8,128)S(1)} %convolution_bitcast_fusion.5), channel_id=1, replica_groups=mesh['section'=8,'tp'=16] {'tp'}, use_global_device_ids=true, to_apply=%region_2.2 | all-reduce | flops 8192 | bytes 65536 | tf_op jit(solution)/shard_map/while/body/eval_jaxpr/psum | solution.py:98
  1195.2 35.9 %collective-permute-done = bf16[128,4096]{1,0:T(8,128)(2,1)S(1)} collective-permute-done((bf16[128,4096]{1,0:T(8,128)(2,1)}, bf16[128,4096]{1,0:T(8,128)(2,1)S(1)}, u32[]{:S(2)}, u32[]{:S(2)}) %collective-permute-start) | collective-permute-done | bytes 1048608 | tf_op jit(solution)/shard_map/while/body/eval_jaxpr/ppermute | solution.py:31
  1281.4 6.7 collective-permute-done.15
  1294.4 55.9 %psum.32 = f32[128,2,32]{0,2,1:T(8,128)S(1)} all-reduce(f32[128,2,32]{0,2,1:T(8,128)S(1)} %convolution_bitcast_fusion.5), channel_id=1, replica_groups=mesh['section'=8,'tp'=16] {'tp'}, use_global_device_ids=true, to_apply=%region_2.2 | all-reduce | flops 8192 | bytes 65536 | tf_op jit(solution)/shard_map/while/body/eval_jaxpr/psum | solution.py:98
  1354.9 35.0 %collective-permute-done = bf16[128,4096]{1,0:T(8,128)(2,1)S(1)} collective-permute-done((bf16[128,4096]{1,0:T(8,128)(2,1)}, bf16[128,4096]{1,0:T(8,128)(2,1)S(1)}, u32[]{:S(2)}, u32[]{:S(2)}) %collective-permute-start) | collective-permute-done | bytes 1048608 | tf_op jit(solution)/shard_map/while/body/eval_jaxpr/ppermute | solution.py:31
  1439.9 6.4 collective-permute-done.15
  1452.7 55.6 %psum.32 = f32[128,2,32]{0,2,1:T(8,128)S(1)} all-reduce(f32[128,2,32]{0,2,1:T(8,128)S(1)} %convolution_bitcast_fusion.5), channel_id=1, replica_groups=mesh['section'=8,'tp'=16] {'tp'}, use_global_device_ids=true, to_apply=%region_2.2 | all-reduce | flops 8192 | bytes 65536 | tf_op jit(solution)/shard_map/while/body/eval_jaxpr/psum | solution.py:98
  1513.0 35.7 %collective-permute-done = bf16[128,4096]{1,0:T(8,128)(2,1)S(1)} collective-permute-done((bf16[128,4096]{1,0:T(8,128)(2,1)}, bf16[128,4096]{1,0:T(8,128)(2,1)S(1)}, u32[]{:S(2)}, u32[]{:S(2)}) %collective-permute-start) | collective-permute-done | bytes 1048608 | tf_op jit(solution)/shard_map/while/body/eval_jaxpr/ppermute | solution.py:31
  1599.0 6.7 collective-permute-done.15
  1612.0 55.9 %psum.32 = f32[128,2,32]{0,2,1:T(8,128)S(1)} all-reduce(f32[128,2,32]{0,2,1:T(8,128)S(1)} %convolution_bitcast_fusion.5), channel_id=1, replica_groups=mesh['section'=8,'tp'=16] {'tp'}, use_global_device_ids=true, to_apply=%region_2.2 | all-reduce | flops 8192 | bytes 65536 | tf_op jit(solution)/shard_map/while/body/eval_jaxpr/psum | solution.py:98
  1672.6 35.0 %collective-permute-done = bf16[128,4096]{1,0:T(8,128)(2,1)S(1)} collective-permute-done((bf16[128,4096]{1,0:T(8,128)(2,1)}, bf16[128,4096]{1,0:T(8,128)(2,1)S(1)}, u32[]{:S(2)}, u32[]{:S(2)}) %collective-permute-start) | collective-permute-done | bytes 1048608 | tf_op jit(solution)/shard_map/while/body/eval_jaxpr/ppermute | solution.py:31
  1770.3 55.6 %psum.32 = f32[128,2,32]{0,2,1:T(8,128)S(1)} all-reduce(f32[128,2,32]{0,2,1:T(8,128)S(1)} %convolution_bitcast_fusion.5), channel_id=1, replica_groups=mesh['section'=8,'tp'=16] {'tp'}, use_global_device_ids=true, to_apply=%region_2.2 | all-reduce | flops 8192 | bytes 65536 | tf_op jit(solution)/shard_map/while/body/eval_jaxpr/psum | solution.py:98
  1829.8 33.1 %psum.29 = f32[2,32]{1,0:T(2,128)} all-reduce(f32[2,32]{1,0:T(2,128)S(1)} %convolution_bitcast_fusion.3), channel_id=1, replica_groups=mesh['section'=8,'tp'=16] {'section'}, use_global_device_ids=true, to_apply=%region_4.5 | all-reduce | flops 64 | bytes 512 | tf_op jit(solution)/shard_map/psum | solution.py:123
  (754 shorter events, 710.4 us)
Async XLA Ops:
  6.5 90.4 %all-reduce.2.cloned.1.call-start = ((), (), s32[]{:S(2)}) async-start(), calls=%async_computation | async-start | bytes 524288 | tf_op jit(solution)/shard_map/psum | solution.py:65
  98.0 141.4 %all-gather.2.cloned.1.call-start = ((), (), s32[]{:S(2)}) async-start(), calls=%async_computation.1 | async-start | bytes 1114112 | tf_op jit(solution)/shard_map/while/body/eval_jaxpr/all_gather | solution.py:93
  98.0 17.6 collective-permute-start
  240.1 158.6 %all-gather.2.cloned.1.call-start = ((), (), s32[]{:S(2)}) async-start(), calls=%async_computation.1 | async-start | bytes 1114112 | tf_op jit(solution)/shard_map/while/body/eval_jaxpr/all_gather | solution.py:93
  240.1 37.5 %collective-permute-start = (bf16[128,4096]{1,0:T(8,128)(2,1)}, bf16[128,4096]{1,0:T(8,128)(2,1)S(1)}, u32[]{:S(2)}, u32[]{:S(2)}) collective-permute-start(bf16[128,4096]{1,0:T(8,128)(2,1)} %get-tuple-element.512), channel_id=1, source_target_pairs={{16,0},{32,16},{48,32},{64,48},{80,64},{96,80},{112,96},{17,1},{33... | collective-permute-start | bytes 3145736 | tf_op jit(solution)/shard_map/while/body/eval_jaxpr/ppermute | solution.py:31
  315.3 12.4 collective-permute-start.14
  399.3 157.9 %all-gather.2.cloned.1.call-start = ((), (), s32[]{:S(2)}) async-start(), calls=%async_computation.1 | async-start | bytes 1114112 | tf_op jit(solution)/shard_map/while/body/eval_jaxpr/all_gather | solution.py:93
  399.3 37.2 %collective-permute-start = (bf16[128,4096]{1,0:T(8,128)(2,1)}, bf16[128,4096]{1,0:T(8,128)(2,1)S(1)}, u32[]{:S(2)}, u32[]{:S(2)}) collective-permute-start(bf16[128,4096]{1,0:T(8,128)(2,1)} %get-tuple-element.512), channel_id=1, source_target_pairs={{16,0},{32,16},{48,32},{64,48},{80,64},{96,80},{112,96},{17,1},{33... | collective-permute-start | bytes 3145736 | tf_op jit(solution)/shard_map/while/body/eval_jaxpr/ppermute | solution.py:31
  474.8 11.7 collective-permute-start.14
  557.8 159.2 %all-gather.2.cloned.1.call-start = ((), (), s32[]{:S(2)}) async-start(), calls=%async_computation.1 | async-start | bytes 1114112 | tf_op jit(solution)/shard_map/while/body/eval_jaxpr/all_gather | solution.py:93
  557.8 37.9 %collective-permute-start = (bf16[128,4096]{1,0:T(8,128)(2,1)}, bf16[128,4096]{1,0:T(8,128)(2,1)S(1)}, u32[]{:S(2)}, u32[]{:S(2)}) collective-permute-start(bf16[128,4096]{1,0:T(8,128)(2,1)} %get-tuple-element.512), channel_id=1, source_target_pairs={{16,0},{32,16},{48,32},{64,48},{80,64},{96,80},{112,96},{17,1},{33... | collective-permute-start | bytes 3145736 | tf_op jit(solution)/shard_map/while/body/eval_jaxpr/ppermute | solution.py:31
  633.9 12.1 collective-permute-start.14
  717.6 157.5 %all-gather.2.cloned.1.call-start = ((), (), s32[]{:S(2)}) async-start(), calls=%async_computation.1 | async-start | bytes 1114112 | tf_op jit(solution)/shard_map/while/body/eval_jaxpr/all_gather | solution.py:93
  717.6 37.0 %collective-permute-start = (bf16[128,4096]{1,0:T(8,128)(2,1)}, bf16[128,4096]{1,0:T(8,128)(2,1)S(1)}, u32[]{:S(2)}, u32[]{:S(2)}) collective-permute-start(bf16[128,4096]{1,0:T(8,128)(2,1)} %get-tuple-element.512), channel_id=1, source_target_pairs={{16,0},{32,16},{48,32},{64,48},{80,64},{96,80},{112,96},{17,1},{33... | collective-permute-start | bytes 3145736 | tf_op jit(solution)/shard_map/while/body/eval_jaxpr/ppermute | solution.py:31
  792.5 11.9 collective-permute-start.14
  875.7 159.0 %all-gather.2.cloned.1.call-start = ((), (), s32[]{:S(2)}) async-start(), calls=%async_computation.1 | async-start | bytes 1114112 | tf_op jit(solution)/shard_map/while/body/eval_jaxpr/all_gather | solution.py:93
  875.7 37.7 %collective-permute-start = (bf16[128,4096]{1,0:T(8,128)(2,1)}, bf16[128,4096]{1,0:T(8,128)(2,1)S(1)}, u32[]{:S(2)}, u32[]{:S(2)}) collective-permute-start(bf16[128,4096]{1,0:T(8,128)(2,1)} %get-tuple-element.512), channel_id=1, source_target_pairs={{16,0},{32,16},{48,32},{64,48},{80,64},{96,80},{112,96},{17,1},{33... | collective-permute-start | bytes 3145736 | tf_op jit(solution)/shard_map/while/body/eval_jaxpr/ppermute | solution.py:31
  952.0 11.6 collective-permute-start.14
  1035.2 157.5 %all-gather.2.cloned.1.call-start = ((), (), s32[]{:S(2)}) async-start(), calls=%async_computation.1 | async-start | bytes 1114112 | tf_op jit(solution)/shard_map/while/body/eval_jaxpr/all_gather | solution.py:93
  1035.2 37.0 %collective-permute-start = (bf16[128,4096]{1,0:T(8,128)(2,1)}, bf16[128,4096]{1,0:T(8,128)(2,1)S(1)}, u32[]{:S(2)}, u32[]{:S(2)}) collective-permute-start(bf16[128,4096]{1,0:T(8,128)(2,1)} %get-tuple-element.512), channel_id=1, source_target_pairs={{16,0},{32,16},{48,32},{64,48},{80,64},{96,80},{112,96},{17,1},{33... | collective-permute-start | bytes 3145736 | tf_op jit(solution)/shard_map/while/body/eval_jaxpr/ppermute | solution.py:31
  1110.5 11.6 collective-permute-start.14
  1193.3 159.1 %all-gather.2.cloned.1.call-start = ((), (), s32[]{:S(2)}) async-start(), calls=%async_computation.1 | async-start | bytes 1114112 | tf_op jit(solution)/shard_map/while/body/eval_jaxpr/all_gather | solution.py:93
  1193.3 37.8 %collective-permute-start = (bf16[128,4096]{1,0:T(8,128)(2,1)}, bf16[128,4096]{1,0:T(8,128)(2,1)S(1)}, u32[]{:S(2)}, u32[]{:S(2)}) collective-permute-start(bf16[128,4096]{1,0:T(8,128)(2,1)} %get-tuple-element.512), channel_id=1, source_target_pairs={{16,0},{32,16},{48,32},{64,48},{80,64},{96,80},{112,96},{17,1},{33... | collective-permute-start | bytes 3145736 | tf_op jit(solution)/shard_map/while/body/eval_jaxpr/ppermute | solution.py:31
  1269.5 11.9 collective-permute-start.14
  1353.0 157.5 %all-gather.2.cloned.1.call-start = ((), (), s32[]{:S(2)}) async-start(), calls=%async_computation.1 | async-start | bytes 1114112 | tf_op jit(solution)/shard_map/while/body/eval_jaxpr/all_gather | solution.py:93
  1353.0 36.9 %collective-permute-start = (bf16[128,4096]{1,0:T(8,128)(2,1)}, bf16[128,4096]{1,0:T(8,128)(2,1)S(1)}, u32[]{:S(2)}, u32[]{:S(2)}) collective-permute-start(bf16[128,4096]{1,0:T(8,128)(2,1)} %get-tuple-element.512), channel_id=1, source_target_pairs={{16,0},{32,16},{48,32},{64,48},{80,64},{96,80},{112,96},{17,1},{33... | collective-permute-start | bytes 3145736 | tf_op jit(solution)/shard_map/while/body/eval_jaxpr/ppermute | solution.py:31
  1427.9 12.0 collective-permute-start.14
  1511.1 159.0 %all-gather.2.cloned.1.call-start = ((), (), s32[]{:S(2)}) async-start(), calls=%async_computation.1 | async-start | bytes 1114112 | tf_op jit(solution)/shard_map/while/body/eval_jaxpr/all_gather | solution.py:93
  1511.1 37.7 %collective-permute-start = (bf16[128,4096]{1,0:T(8,128)(2,1)}, bf16[128,4096]{1,0:T(8,128)(2,1)S(1)}, u32[]{:S(2)}, u32[]{:S(2)}) collective-permute-start(bf16[128,4096]{1,0:T(8,128)(2,1)} %get-tuple-element.512), channel_id=1, source_target_pairs={{16,0},{32,16},{48,32},{64,48},{80,64},{96,80},{112,96},{17,1},{33... | collective-permute-start | bytes 3145736 | tf_op jit(solution)/shard_map/while/body/eval_jaxpr/ppermute | solution.py:31
  1670.6 157.5 %all-gather.2.cloned.1.call-start = ((), (), s32[]{:S(2)}) async-start(), calls=%async_computation.1 | async-start | bytes 1114112 | tf_op jit(solution)/shard_map/while/body/eval_jaxpr/all_gather | solution.py:93
  1670.6 36.9 %collective-permute-start = (bf16[128,4096]{1,0:T(8,128)(2,1)}, bf16[128,4096]{1,0:T(8,128)(2,1)S(1)}, u32[]{:S(2)}, u32[]{:S(2)}) collective-permute-start(bf16[128,4096]{1,0:T(8,128)(2,1)} %get-tuple-element.512), channel_id=1, source_target_pairs={{16,0},{32,16},{48,32},{64,48},{80,64},{96,80},{112,96},{17,1},{33... | collective-permute-start | bytes 3145736 | tf_op jit(solution)/shard_map/while/body/eval_jaxpr/ppermute | solution.py:31
  1745.6 12.0 collective-permute-start.14
  (203 other events, 3639.6 us)
Sparse Core Ops, SparseCore 0:
  10.5 86.3 all-reduce.1
  178.0 46.2 all-gather.1
  337.3 46.3 all-gather.1
  496.2 46.3 all-gather.1
  655.9 45.4 all-gather.1
  814.1 46.0 all-gather.1
  973.2 45.7 all-gather.1
  1131.7 46.0 all-gather.1
  1291.3 45.2 all-gather.1
  1449.6 45.8 all-gather.1
  1608.9 45.2 all-gather.1
  1767.2 45.8 all-gather.1
